TPU v7x, 32 devices: a whole 2x2x4 slice. The times are simulated.
32 devices in a mesh: groups: 2 (over y), expert: 4 (over z), dp: 4 (over x, core).
Axes of the slice: x: 2, y: 2, z: 4, core: 2. Of those that a mesh axis runs over, the one named last changes fastest.
Arguments:
- tokens: bfloat16 [512, 6144], P(('groups', 'expert'), 'dp'), parts along dimension 0, may hold values from -6 to 6
- expert_ids: int32 [512, 8], P(('groups', 'expert')), parts along dimension 0, may hold values from 0 to 31, all different within a row; in each aligned block of 64 rows (0 to 63, 64 to 127, ...) at most 32 rows name the same one
- scores: float32 [512, 8], P(('groups', 'expert')), parts along dimension 0, may hold values from -8 to 8
- w_gate: bfloat16 [32, 6144, 1024], P('expert', 'dp'), may hold values from -0.078125 to 0.078125
- w_up: bfloat16 [32, 6144, 1024], P('expert', 'dp'), may hold values from -0.078125 to 0.078125
- w_down: bfloat16 [32, 1024, 6144], P('expert', None, 'dp'), may hold values from -0.1875 to 0.1875
Outputs:
- mixed: bfloat16 [512, 6144], P(('groups', 'expert'), 'dp'), parts along dimension 0
There are 2 independent parts, one for each index of `groups`. A program takes and returns all parts, laid end to end along the dimension named above; an argument that names none is the same for every part. Nothing has to cross between parts.
Inputs may be any that keep to these rules, and one draw needn't show every extreme that they name: `expert_ids`: each row names 8 different experts; among the rows of one index of expert (aligned blocks of 64 rows) no expert is named by more than 32 rows, a bound that some block reaches.
All inputs are finite; a program needn't handle non-finite values.
Results may differ from a plain program's by a relative error of at most 0.024.
Values may be sent and summed in bfloat16 or wider, within the bound.
A program may use at most 128 MiB of HBM per device.

v0:
```python
import jax
import jax.numpy as jnp
from jax import lax
from jax.sharding import PartitionSpec as P


def on_device(tokens, expert_ids, scores, w_gate, w_up, w_down):
    n_owner = lax.axis_size("expert")
    tok_rows, local_width = tokens.shape
    top = expert_ids.shape[1]
    experts_here = w_gate.shape[0]
    experts_all = experts_here * n_owner
    capacity = 2 * tok_rows * top // experts_all
    flat_ids = expert_ids.reshape(-1)
    onehot = (flat_ids[:, None] == jnp.arange(experts_all, dtype=jnp.int32)[None, :]).astype(
        jnp.int32
    )
    earlier = jnp.cumsum(onehot, axis=0) - onehot
    rank = jnp.sum(earlier * onehot, axis=1)
    slots = flat_ids * capacity + rank
    place = jnp.any(
        jnp.arange(experts_all * capacity, dtype=jnp.int32)[:, None, None]
        == slots.reshape(tok_rows, top)[None],
        axis=2,
    )
    buffer = jnp.dot(place.astype(jnp.bfloat16), tokens, preferred_element_type=jnp.float32).astype(
        jnp.bfloat16
    )
    buffer = buffer.reshape(n_owner, experts_here, capacity, local_width)
    received = lax.all_to_all(buffer, "expert", split_axis=0, concat_axis=0, tiled=True)
    gate_part = jnp.einsum("sjcd,jdh->sjch", received, w_gate, preferred_element_type=jnp.float32)
    up_part = jnp.einsum("sjcd,jdh->sjch", received, w_up, preferred_element_type=jnp.float32)
    gate = lax.psum_scatter(
        gate_part.astype(jnp.bfloat16), "dp", scatter_dimension=3, tiled=True
    ).astype(jnp.float32)
    up = lax.psum_scatter(
        up_part.astype(jnp.bfloat16), "dp", scatter_dimension=3, tiled=True
    ).astype(jnp.float32)
    share = (jax.nn.silu(gate) * up).astype(jnp.bfloat16)
    hidden = lax.all_gather(share, "dp", axis=3, tiled=True)
    expert_out = jnp.einsum(
        "sjch,jhd->sjcd", hidden, w_down, preferred_element_type=jnp.float32
    ).astype(jnp.bfloat16)
    returned = lax.all_to_all(expert_out, "expert", split_axis=0, concat_axis=0, tiled=True)
    returned = returned.reshape(experts_all * capacity, local_width)
    picked = returned[slots].reshape(tok_rows, top, local_width).astype(jnp.float32)
    affinity = jax.nn.sigmoid(scores)
    weights = 2.5 * affinity / jnp.sum(affinity, axis=1, keepdims=True)
    return jnp.einsum("tk,tkd->td", weights, picked).astype(jnp.bfloat16)


def solution(mesh):
    in_specs = (
        P(("groups", "expert"), "dp"),
        P(("groups", "expert"), None),
        P(("groups", "expert"), None),
        P("expert", "dp", None),
        P("expert", "dp", None),
        P("expert", None, "dp"),
    )
    out_specs = P(("groups", "expert"), "dp")
    return jax.shard_map(
        on_device, mesh=mesh, in_specs=in_specs, out_specs=out_specs, check_vma=False
    )
```

profile of v0, /device:TPU:0, one launch (start us, length us, event | category | flops | bytes accessed | tf_op | source)
XLA Modules:
  0.0 292.5 jit_solution(15262649235627956736)
XLA Ops:
  6.5 0.8 copy.22
  7.3 0.1 eq.43
  7.5 1.2 reduce-window.6
  8.7 0.2 slice_reduce_fusion
  9.0 0.1 fusion.32
  9.1 0.1 reduce_sum.24
  9.2 0.7 fusion.14
  9.9 1.0 convolution_convert_fusion
  10.9 76.8 %all_to_all.10 = bf16[4,8,32,1536]{3,2,1,0:T(8,128)(2,1)S(1)} all-to-all(bf16[4,8,32,1536]{3,2,1,0:T(8,128)(2,1)S(1)} %bitcast.65), channel_id=1, replica_groups=mesh['groups'=2,'expert'=4,'dp'=4] {'expert'}, dimensions={0} | all-to-all | bytes 6291456 | tf_op jit(solution)/shard_map/all_to_all | solution.py:30
  87.8 12.9 %convert_bitcast_fusion.1 = bf16[4,8,32,1024]{3,2,0,1:T(8,128)(2,1)} fusion(bf16[8,1536,1024]{2,1,0:T(8,128)(2,1)} %param.9, bf16[4,8,32,1536]{3,2,1,0:T(8,128)(2,1)S(1)} %all_to_all.10), kind=kOutput, calls=%fused_computation.13 | convolution fusion | flops 3222274048 | bytes 30408704 | tf_op jit(solution)/shard_map/sjcd,jdh->sjch/dot_general | solution.py:31
  100.8 13.9 %convert_bitcast_fusion = bf16[4,8,32,1024]{3,2,0,1:T(8,128)(2,1)} fusion(bf16[8,1536,1024]{2,1,0:T(8,128)(2,1)} %param.10, bf16[4,8,32,1536]{3,2,1,0:T(8,128)(2,1)S(1)} %all_to_all.10), kind=kOutput, calls=%fused_computation.12 | convolution fusion | flops 3222274048 | bytes 30408704 | tf_op jit(solution)/shard_map/sjcd,jdh->sjch/dot_general | solution.py:32
  114.7 0.2 all-gather.2.cloned.1.call-start
  114.9 16.4 %reduce-scatter.3.cloned.1.call-done = bf16[4,8,32,256]{3,2,0,1:T(8,128)(2,1)} async-done(((bf16[4,8,32,1024]{3,2,0,1:T(8,128)(2,1)}), bf16[4,8,32,256]{3,2,0,1:T(8,128)(2,1)}) %reduce-scatter.3.cloned.1.call-update) | async-done | bytes 524304 | tf_op jit(solution)/shard_map/reduce_scatter | solution.py:33
  131.4 33.7 %reduce-scatter.5.cloned.1.call-done = bf16[4,8,32,256]{3,2,0,1:T(8,128)(2,1)} async-done(((bf16[4,8,32,1024]{3,2,0,1:T(8,128)(2,1)}), bf16[4,8,32,256]{3,2,0,1:T(8,128)(2,1)}) %reduce-scatter.5.cloned.1.call-update) | async-done | bytes 524304 | tf_op jit(solution)/shard_map/reduce_scatter | solution.py:36
  165.1 2.3 fusion.29
  167.4 23.0 %all-gather.2.cloned.1.call-done = bf16[4,8,32,1024]{3,2,0,1:T(8,128)(2,1)} async-done(((bf16[4,8,32,256]{3,2,0,1:T(8,128)(2,1)}), bf16[4,8,32,1024]{3,2,0,1:T(8,128)(2,1)}) %all-gather.2.cloned.1.call-update) | async-done | bytes 2097168 | tf_op jit(solution)/shard_map/all_gather | solution.py:40
  190.4 12.3 %fusion.9 = bf16[4,8,32,1536]{3,2,0,1:T(8,128)(2,1)S(1)} fusion(bf16[4,8,32,1024]{3,2,0,1:T(8,128)(2,1)} %all-gather.2.cloned.1.call-done, bf16[8,1024,1536]{2,1,0:T(8,128)(2,1)} %param.11), kind=kOutput, calls=%fused_computation.9 | convolution fusion | flops 3222798336 | bytes 30408704 | tf_op jit(solution)/shard_map/sjch,jhd->sjcd/dot_general | solution.py:41
  202.7 1.9 copy.28
  204.6 4.7 %all-to-all-start.1 = ((bf16[4,8,32,1536]{3,2,1,0:T(8,128)(2,1)}), bf16[4,8,32,1536]{3,2,1,0:T(8,128)(2,1)S(1)}, u32[]{:S(2)}, u32[]{:S(2)}) async-start(bf16[4,8,32,1536]{3,2,1,0:T(8,128)(2,1)} %copy.28), calls=%async_computation.3 | async-start | bytes 6291456 | tf_op jit(solution)/shard_map/all_to_all | solution.py:44
  209.4 0.1 copy.32
  209.6 70.8 %all-to-all-done.1 = bf16[4,8,32,1536]{3,2,1,0:T(8,128)(2,1)S(1)} async-done(((bf16[4,8,32,1536]{3,2,1,0:T(8,128)(2,1)}), bf16[4,8,32,1536]{3,2,1,0:T(8,128)(2,1)S(1)}, u32[]{:S(2)}, u32[]{:S(2)}) %all-to-all-start.1) | async-done | bytes 3145760 | tf_op jit(solution)/shard_map/all_to_all | solution.py:44
  280.4 3.0 %gather_fusion = bf16[512,1536]{1,0:T(8,128)(2,1)} fusion(bf16[1024,1536]{1,0:T(8,128)(2,1)S(1)} %bitcast.64, s32[1024]{0:T(1024)S(1)} %pad_clamp_fusion), kind=kCustom, calls=%fused_computation | custom fusion | bytes 3147776 | tf_op jit(solution)/shard_map/gather | solution.py:46
  283.3 2.0 fusion.23
  285.3 0.7 copy.45
  (21 shorter events, 0.4 us)
Async XLA Ops:
  6.5 3.4 %copy-start = (bf16[64,1536]{1,0:T(8,128)(2,1)S(1)}, bf16[64,1536]{1,0:T(8,128)(2,1)}, u32[]{:S(2)}) copy-start(bf16[64,1536]{1,0:T(8,128)(2,1)} %param.6) | copy-start | bytes 589828
  6.5 124.8 %reduce-scatter.3.cloned.1.call-start = ((), (), s32[]{:S(2)}) async-start(), calls=%async_computation.4 | async-start | bytes 2621440 | tf_op jit(solution)/shard_map/reduce_scatter | solution.py:33
  100.7 64.3 %reduce-scatter.5.cloned.1.call-start = ((), (), s32[]{:S(2)}) async-start(), calls=%async_computation.5 | async-start | bytes 2621440 | tf_op jit(solution)/shard_map/reduce_scatter | solution.py:36
  114.7 75.7 %all-gather.2.cloned.1.call-start = ((), (), s32[]{:S(2)}) async-start(), calls=%async_computation.6 | async-start | bytes 2621440 | tf_op jit(solution)/shard_map/all_gather | solution.py:40
  204.6 4.8 %copy-start.2 = (f32[64,8]{0,1:T(8,128)S(1)}, f32[64,8]{0,1:T(8,128)}, u32[]{:S(2)}) copy-start(f32[64,8]{0,1:T(8,128)} %param.8) | copy-start | bytes 6148
  204.6 75.8 %all-to-all-start.1 = ((bf16[4,8,32,1536]{3,2,1,0:T(8,128)(2,1)}), bf16[4,8,32,1536]{3,2,1,0:T(8,128)(2,1)S(1)}, u32[]{:S(2)}, u32[]{:S(2)}) async-start(bf16[4,8,32,1536]{3,2,1,0:T(8,128)(2,1)} %copy.28), calls=%async_computation.3 | async-start | bytes 6291456 | tf_op jit(solution)/shard_map/all_to_all | solution.py:44
  280.4 5.6 %copy-start.1 = (bf16[64,1536]{1,0:T(8,128)(2,1)S(1)}, bf16[64,1536]{1,0:T(8,128)(2,1)}, u32[]{:S(2)}) copy-start(bf16[64,1536]{1,0:T(8,128)(2,1)} %param.6) | copy-start | bytes 589828
Sparse Core Ops, SparseCore 0:
  100.9 30.4 reduce-scatter.2
  133.9 31.1 reduce-scatter.4
  167.6 22.7 all-gather.1
where the time goes:
time: 293 us
  waiting for transfers between devices  144 us (49%)
  blocking collectives  76.8 us (26%)
  matrix products  42.1 us (14%)
  between operations  13.2 us (5%)
  local copies, waits for them, and re-layouts  7.05 us (2%)
  starting transfers between devices  5 us (2%)
  other arithmetic  4.42 us (2%)
    all_to_all x1, blocking collectives, on_device(): lax.all_to_all(buffer, 'expert', split_axis=0, concat_axis=0, tiled=True)  76.8 us
    all_to_all x1, waiting for transfers between devices, on_device(): lax.all_to_all(expert_out, 'expert', split_axis=0, concat_axis=0, tiled=T...  70.8 us
    reduce_scatter x1, waiting for transfers between devices, on_device(): lax.psum_scatter(up_part.astype(jnp.bfloat16), 'dp', scatter_dimension=3,...  33.7 us
    all_gather x1, waiting for transfers between devices, on_device(): hidden = lax.all_gather(share, 'dp', axis=3, tiled=True)  23 us
    reduce_scatter x1, waiting for transfers between devices, on_device(): lax.psum_scatter(gate_part.astype(jnp.bfloat16), 'dp', scatter_dimension=...  16.4 us
    dot_general x1, matrix products, on_device(): jnp.einsum('sjcd,jdh->sjch', received, w_up, preferred_element_type=jnp.f...  13.9 us
    dot_general x1, matrix products, on_device(): jnp.einsum('sjcd,jdh->sjch', received, w_gate, preferred_element_type=jnp...  12.9 us
    dot_general x1, matrix products, on_device(): jnp.einsum('sjch,jhd->sjcd', hidden, w_down, preferred_element_type=jnp.f...  12.3 us
  transfers between devices with their start and end apart: 4, of which 4 were waited for; matrix products, arithmetic and copies ran while one was open for 5% of the time, Pallas kernels for 0%

commit v1 on v0

v1 whole, which is shorter than its diff:
```python
import functools

import jax
import jax.numpy as jnp
from jax import lax
from jax.experimental import pallas as pl
from jax.experimental.pallas import tpu as pltpu
from jax.sharding import PartitionSpec as P

MESH = pl.DeviceIdType.MESH
F32, BF16 = jnp.float32, jnp.bfloat16
LAGS = (0, 1, 2, 3, 4)


def dot(a, b, dims=((1,), (0,))):
    return lax.dot_general(a, b, (dims, ((), ())), preferred_element_type=F32)


def remote(src, dst, send, recv, **where):
    return pltpu.make_async_remote_copy(
        src_ref=src, dst_ref=dst, send_sem=send, recv_sem=recv,
        device_id=where, device_id_type=MESH,
    )


def tile_of(size):
    for tile in (512, 384, 256, 128):
        if size % tile == 0:
            return tile
    return size


def kernel(dims, tok_ref, ids_ref, sco_ref, wg_hbm, wu_hbm, wd_hbm, out_ref,
           wg, wu, wd, xall, meta, slot_c, wgt_c, rows, s1, r1, keep, s2, r2, hid, acc,
           rs_s, rs_r, rs_l,
           wsem, ag_s, ag_r, p_s, p_r, q_s, q_r, h_s, h_r, f_s, f_r, t_s, t_r):
    E, DP, EL, NCH, G, CAP, NB = dims
    M = DP // 2
    tok, width = tok_ref.shape
    H = wg.shape[2]
    hb = H // DP
    R, T = G * CAP, G * tok
    N = EL * NCH
    ct = tile_of(width)
    e = lax.axis_index("expert")
    d = lax.axis_index("dp")
    x, c = lax.div(d, 2), lax.rem(d, 2)
    mate = 2 * x + 1 - c
    has_left, has_right = e > 0, e < E - 1

    def across(k):
        return lax.rem(x + k, M)

    def source(k):
        return lax.rem(x + M - k, M)

    def w_gu(j, slot):
        return (pltpu.make_async_copy(wg_hbm.at[j], wg.at[slot], wsem.at[0, slot]),
                pltpu.make_async_copy(wu_hbm.at[j], wu.at[slot], wsem.at[1, slot]))

    def w_d(j, slot):
        return pltpu.make_async_copy(wd_hbm.at[j], wd.at[slot], wsem.at[2, slot])

    for j in range(NB):
        for copy in w_gu(j, j):
            copy.start()
    for j in range(NB):
        w_d(j, j).start()

    barrier = pltpu.get_barrier_semaphore()

    @pl.when(has_left)
    def _():
        pl.semaphore_signal(barrier, inc=1, device_id={"expert": e - 1}, device_id_type=MESH)

    @pl.when(has_right)
    def _():
        pl.semaphore_signal(barrier, inc=1, device_id={"expert": e + 1}, device_id_type=MESH)

    pl.semaphore_signal(barrier, inc=1, device_id={"dp": mate}, device_id_type=MESH)
    for k in range(1, M):
        pl.semaphore_signal(
            barrier, inc=1, device_id={"dp": 2 * across(k) + c}, device_id_type=MESH)

    n_exp = E * EL
    affinity = 1.0 / (1.0 + jnp.exp(-sco_ref[...]))
    weights = 2.5 * affinity / jnp.sum(affinity, axis=0, keepdims=True)
    number = lax.broadcasted_iota(jnp.int32, (n_exp, tok), 0)
    routed = jnp.zeros((n_exp, tok), F32)
    weight = jnp.zeros((n_exp, tok), F32)
    for k in range(ids_ref.shape[0]):
        hit = ids_ref[k:k + 1, :] == number
        routed = routed + jnp.where(hit, 1.0, 0.0)
        weight = weight + jnp.where(hit, weights[k:k + 1, :], 0.0)
    earlier = (lax.broadcasted_iota(jnp.int32, (tok, tok), 0)
               < lax.broadcasted_iota(jnp.int32, (tok, tok), 1))
    rank = dot(routed.astype(BF16), jnp.where(earlier, 1.0, 0.0).astype(BF16))
    base = (lax.rem(e, G) * CAP).astype(F32)
    meta[e, :, :tok] = jnp.where(routed > 0.5, rank + base, -1.0)
    meta[e, :, tok:] = weight
    xall[e] = tok_ref[...]

    pl.semaphore_wait(barrier, M + has_left.astype(jnp.int32) + has_right.astype(jnp.int32))

    def gather_to(s, side, target):
        return (remote(meta.at[s], meta.at[s], ag_s.at[side, 0, s], ag_r.at[0, s], expert=target),
                remote(xall.at[s], xall.at[s], ag_s.at[side, 1, s], ag_r.at[1, s], expert=target))

    def start_right(s):
        @pl.when(has_right)
        def _():
            for copy in gather_to(s, 0, e + 1):
                copy.start()

    def start_left(s):
        @pl.when(has_left)
        def _():
            for copy in gather_to(s, 1, e - 1):
                copy.start()

    start_right(e)
    start_left(e)

    def gather_step(k, carry):
        @pl.when(e - k >= 0)
        def _():
            for copy in gather_to(e - k, 0, e):
                copy.wait_recv()
            start_right(e - k)

        @pl.when(e + k <= E - 1)
        def _():
            for copy in gather_to(e + k, 1, e):
                copy.wait_recv()
            start_left(e + k)

        return carry

    lax.fori_loop(1, E, gather_step, 0)

    for s in range(E):
        lanes = slice((s % G) * tok, (s % G + 1) * tok)
        own = meta[s, pl.ds(e * EL, EL), :]
        slot_c[s // G, :, lanes] = own[:, :tok]
        wgt_c[s // G, :, lanes] = own[:, tok:]
    acc[...] = jnp.zeros_like(acc)

    def split(i):
        if NCH == 1:
            return i, 0
        return lax.div(i, NCH), lax.rem(i, NCH)

    def taken(j, q):
        return (slot_c[q, pl.ds(j, 1), :]
                == lax.broadcasted_iota(jnp.int32, (R, T), 0).astype(F32))

    def pair_copy(i):
        return remote(s1.at[i], r1.at[i], p_s.at[i], p_r.at[i], dp=mate)

    def sum_copy(i, k):
        return remote(s2.at[i, across(k)], r2.at[i, x], q_s.at[i, k], q_r.at[i, k],
                      dp=2 * across(k) + c)

    def share_copy(i, k):
        return remote(hid.at[i, d], hid.at[i, d], h_s.at[i, k], h_r.at[i, k],
                      dp=2 * across(k) + c)

    def mate_copy(i, k):
        block = 2 * source(k) + c
        return remote(hid.at[i, block], hid.at[i, block], f_s.at[i, k], f_r.at[i, k], dp=mate)

    def stage_a(i):
        j, q = split(i)
        slot = lax.rem(j, NB)

        def load():
            for copy in w_gu(j, slot):
                copy.wait()

        if NCH == 1:
            load()
        else:
            pl.when(q == 0)(load)
        pick = jnp.where(taken(j, q), 1.0, 0.0).astype(BF16)
        for at in range(0, width, ct):
            xq = xall[pl.ds(q * G, G), :, at:at + ct].reshape(T, ct)
            rows[:, at:at + ct] = dot(pick, xq).astype(BF16)

        def block(m, core):
            cols = pl.ds(pl.multiple_of((2 * m + core) * hb, hb), hb)
            xr = rows[...]
            return dot(xr, wg[slot, :, cols]), dot(xr, wu[slot, :, cols])

        for m in range(M):
            g, u = block(m, 1 - c)
            s1[i, m, :, :hb] = g.astype(BF16)
            s1[i, m, :, hb:] = u.astype(BF16)
        pair_copy(i).start()
        for m in range(M):
            g, u = block(m, c)
            keep[i, m, :, :hb] = g
            keep[i, m, :, hb:] = u

        @pl.when((q == NCH - 1) & (j + NB < EL))
        def _():
            for copy in w_gu(j + NB, slot):
                copy.start()

    def stage_b(i):
        pair_copy(i).wait_recv()
        for k in range(1, M):
            to = across(k)
            s2[i, to] = (keep[i, to] + r1[i, to].astype(F32)).astype(BF16)
            sum_copy(i, k).start()
        keep[i, x] = keep[i, x] + r1[i, x].astype(F32)

    def stage_c(i):
        total = keep[i, x]
        for k in range(1, M):
            sum_copy(i, k).wait_recv()
            total = total + r2[i, source(k)].astype(F32)
        g, u = total[:, :hb], total[:, hb:]
        hid[i, d] = (g / (1.0 + jnp.exp(-g)) * u).astype(BF16)
        for k in range(1, M):
            share_copy(i, k).start()
        mate_copy(i, 0).start()

    def stage_d(i):
        for k in range(1, M):
            share_copy(i, k).wait_recv()
            mate_copy(i, k).start()

    def stage_e(i):
        j, q = split(i)
        slot = lax.rem(j, NB)

        def load():
            w_d(j, slot).wait()

        if NCH == 1:
            load()
        else:
            pl.when(q == 0)(load)
        for k in range(M):
            mate_copy(i, k).wait_recv()
        hit = taken(j, q)
        scale = jnp.sum(jnp.where(hit, wgt_c[q, pl.ds(j, 1), :], 0.0), axis=1, keepdims=True)
        pick = jnp.where(hit, 1.0, 0.0).astype(BF16)
        hidden = jnp.concatenate([hid[i, b] for b in range(DP)], axis=1)
        for at in range(0, width, ct):
            out = (dot(hidden, wd[slot, :, at:at + ct]) * scale).astype(BF16)
            add = dot(pick, out, ((0,), (0,))).reshape(G, tok, ct)
            acc[pl.ds(q * G, G), :, at:at + ct] += add

        @pl.when((q == NCH - 1) & (j + NB < EL))
        def _():
            w_d(j + NB, slot).start()

    stages = (stage_a, stage_b, stage_c, stage_d, stage_e)

    def step(i, carry):
        for stage, lag in zip(stages, LAGS):
            @pl.when((i >= lag) & (i < N + lag))
            def _(stage=stage, lag=lag):
                stage(i - lag)
        return carry

    lax.fori_loop(0, N + LAGS[-1], step, 0)

    def tail_right(s, target):
        return remote(rs_s.at[s], rs_r.at[s], t_s.at[s], t_r.at[0, s], expert=target)

    def tail_left(s, target):
        return remote(rs_s.at[s], rs_l.at[s], t_s.at[s], t_r.at[1, s], expert=target)

    def tail_step(t, carry):
        far, near = E - 1 - t, t

        @pl.when(far > e)
        def _():
            @pl.when(has_left)
            def _():
                tail_right(far, e).wait_recv()
                rs_s[far] = (acc[far] + rs_r[far].astype(F32)).astype(BF16)

            @pl.when(jnp.logical_not(has_left))
            def _():
                rs_s[far] = acc[far].astype(BF16)

            tail_right(far, e + 1).start()

        @pl.when(near < e)
        def _():
            @pl.when(has_right)
            def _():
                tail_left(near, e).wait_recv()
                rs_s[near] = (acc[near] + rs_l[near].astype(F32)).astype(BF16)

            @pl.when(jnp.logical_not(has_right))
            def _():
                rs_s[near] = acc[near].astype(BF16)

            tail_left(near, e - 1).start()

        return carry

    lax.fori_loop(0, E - 1, tail_step, 0)

    @pl.when(has_left)
    def _():
        tail_right(e, e).wait_recv()
        acc[e] = acc[e] + rs_r[e].astype(F32)

    @pl.when(has_right)
    def _():
        tail_left(e, e).wait_recv()
        acc[e] = acc[e] + rs_l[e].astype(F32)

    out_ref[...] = acc[e].astype(BF16)

    def drain_line(s, carry):
        @pl.when((s <= e) & has_right)
        def _():
            for copy in gather_to(s, 0, e):
                copy.wait_send()

        @pl.when((s >= e) & has_left)
        def _():
            for copy in gather_to(s, 1, e):
                copy.wait_send()

        @pl.when(s != e)
        def _():
            tail_right(s, e).wait_send()

        return carry

    lax.fori_loop(0, E, drain_line, 0)

    def drain_item(i, carry):
        pair_copy(i).wait_send()
        mate_copy(i, 0).wait_send()
        for k in range(1, M):
            sum_copy(i, k).wait_send()
            share_copy(i, k).wait_send()
            mate_copy(i, k).wait_send()
        return carry

    lax.fori_loop(0, N, drain_item, 0)


def on_device(tokens, expert_ids, scores, w_gate, w_up, w_down):
    E, DP = lax.axis_size("expert"), lax.axis_size("dp")
    tok, width = tokens.shape
    top = expert_ids.shape[1]
    EL, _, H = w_gate.shape
    n_exp = E * EL
    CAP = 2 * tok * top // n_exp
    G = min(E, 4)
    NCH = E // G
    NB = min(3, EL)
    M, hb, R, N = DP // 2, H // DP, G * CAP, EL * NCH
    vmem, dma = pltpu.VMEM, pltpu.SemaphoreType.DMA
    scratch = [
        vmem((NB, width, H), BF16), vmem((NB, width, H), BF16), vmem((NB, H, width), BF16),
        vmem((E, tok, width), BF16), vmem((E, n_exp, 2 * tok), F32),
        vmem((NCH, EL, G * tok), F32), vmem((NCH, EL, G * tok), F32),
        vmem((R, width), BF16),
        vmem((N, M, R, 2 * hb), BF16), vmem((N, M, R, 2 * hb), BF16),
        vmem((N, M, R, 2 * hb), F32),
        vmem((N, M, R, 2 * hb), BF16), vmem((N, M, R, 2 * hb), BF16),
        vmem((N, DP, R, hb), BF16),
        vmem((E, tok, width), F32),
        vmem((E, tok, width), BF16), vmem((E, tok, width), BF16), vmem((E, tok, width), BF16),
        dma((3, NB)), dma((2, 2, E)), dma((2, E)),
        dma((N,)), dma((N,)), dma((N, M)), dma((N, M)), dma((N, M)), dma((N, M)),
        dma((N, M)), dma((N, M)), dma((E,)), dma((2, E)),
    ]
    whole = pl.BlockSpec(memory_space=pltpu.VMEM)
    hbm = pl.BlockSpec(memory_space=pl.ANY)
    return pl.pallas_call(
        functools.partial(kernel, (E, DP, EL, NCH, G, CAP, NB)),
        out_shape=jax.ShapeDtypeStruct((tok, width), BF16),
        in_specs=[whole] * 3 + [hbm] * 3,
        out_specs=whole,
        scratch_shapes=scratch,
        compiler_params=pltpu.CompilerParams(
            collective_id=0, has_side_effects=True, vmem_limit_bytes=60 * 2**20),
        name="routed_experts",
    )(tokens, expert_ids.T, scores.T, w_gate, w_up, w_down)


def solution(mesh):
    in_specs = (
        P(("groups", "expert"), "dp"),
        P(("groups", "expert"), None),
        P(("groups", "expert"), None),
        P("expert", "dp", None),
        P("expert", "dp", None),
        P("expert", None, "dp"),
    )
    out_specs = P(("groups", "expert"), "dp")
    return jax.shard_map(
        on_device, mesh=mesh, in_specs=in_specs, out_specs=out_specs, check_vma=False
    )
```

time: 293 us -> 91.8 us (0.31)
  waiting for transfers between devices: 144 us -> 0 us
  Pallas kernels: 0 us -> 90 us
  blocking collectives: 76.8 us -> 0 us
  matrix products: 42.1 us -> 0 us
  between operations: 13.2 us -> 0.01 us
  local copies, waits for them, and re-layouts: 7.05 us -> 1.62 us
  starting transfers between devices: 5 us -> 0 us
  other arithmetic: 4.42 us -> 0 us
    pallas_call x0 -> x1, Pallas kernels: none -> 90 us  [on_device(): pl.pallas_call(functools.partial(kernel, (E, DP, EL, NCH, G, CAP, NB)), o...]
    all_to_all x1 -> x0, blocking collectives: 76.8 us -> none  [on_device(): lax.all_to_all(buffer, 'expert', split_axis=0, concat_axis=0, tiled=True)]
    all_to_all x1 -> x0, waiting for transfers between devices: 70.8 us -> none  [on_device(): lax.all_to_all(expert_out, 'expert', split_axis=0, concat_axis=0, tiled=T...]
    reduce_scatter x2 -> x0, waiting for transfers between devices: 50.1 us -> none  [the longest x1 33.7 us: on_device(): lax.psum_scatter(up_part.astype(jnp.bfloat16), 'dp', scatter_dimension=3,...]
    dot_general x5 -> x0, matrix products: 42.1 us -> none  [the longest x1 13.9 us: on_device(): jnp.einsum('sjcd,jdh->sjch', received, w_up, preferred_element_type=jnp.f...]
    all_gather x1 -> x0, waiting for transfers between devices: 23 us -> none  [on_device(): hidden = lax.all_gather(share, 'dp', axis=3, tiled=True)]
    all_to_all x1 -> x0, starting transfers between devices: 4.73 us -> none  [on_device(): lax.all_to_all(expert_out, 'expert', split_axis=0, concat_axis=0, tiled=T...]
    gather x1 -> x0, local copies, waits for them, and re-layouts: 2.95 us -> none  [on_device(): returned[slots].reshape(tok_rows, top, local_width).astype(jnp.float32)]
  transfers between devices with their start and end apart: 4 -> 0, of which waited for: 4 -> 0; matrix products, arithmetic and copies ran while one was open for 5% -> 0% of each run, Pallas kernels for 0% -> 0%
where the time goes in v1:
time: 91.8 us; the launch traced here: 91.7 us
  Pallas kernels  90 us (98%)
  local copies, waits for them, and re-layouts  1.62 us (2%)
    pallas_call x1, Pallas kernels, on_device(): pl.pallas_call(functools.partial(kernel, (E, DP, EL, NCH, G, CAP, NB)), o...  90 us

profile of v1, /device:TPU:0, one launch (start us, length us, event | category | flops | bytes accessed | tf_op | source)
XLA Modules:
  0.0 91.7 jit_solution(12015728471021232921)
XLA Ops:
  0.0 90.0 %routed_experts.1 = bf16[64,1536]{1,0:T(8,128)(2,1)} custom-call(bf16[64,1536]{1,0:T(8,128)(2,1)} %tok_ref.1, s32[8,64]{1,0:T(8,128)} %bitcast.2, f32[8,64]{1,0:T(8,128)} %bitcast.3, bf16[8,1536,1024]{2,1,0:T(8,128)(2,1)} %wg_hbm.1, bf16[8,1536,1024]{2,1,0:T(8,128)(2,1)} %wu_hbm.1, bf16[8,1024,1536]{2,1,0:T(8,128)(2,1)} %wd_hbm.1), custom_call_target="tpu_custom_call" | custom-call | tf_op jit(solution)/shard_map/routed_experts/pallas_call | solution.py:381
  90.0 1.6 %copy.8 = bf16[64,1536]{1,0:T(8,128)(2,1)} copy(bf16[64,1536]{1,0:T(8,128)(2,1)} %routed_experts.1) | data formatting | bytes 393216

commit v2 on v1

v2 whole, which is shorter than its diff:
```python
import functools

import jax
import jax.numpy as jnp
from jax import lax
from jax.experimental import pallas as pl
from jax.experimental.pallas import tpu as pltpu
from jax.sharding import PartitionSpec as P

MESH = pl.DeviceIdType.MESH
F32, BF16 = jnp.float32, jnp.bfloat16
LAGS = (0, 1, 2, 3, 4)


def dot(a, b, dims=((1,), (0,))):
    return lax.dot_general(a, b, (dims, ((), ())), preferred_element_type=F32)


def remote(src, dst, send, recv, **where):
    return pltpu.make_async_remote_copy(
        src_ref=src, dst_ref=dst, send_sem=send, recv_sem=recv,
        device_id=where, device_id_type=MESH,
    )


def tile_of(size):
    for tile in (512, 384, 256, 128):
        if size % tile == 0:
            return tile
    return size


def kernel(dims, tok_ref, ids_ref, sco_ref, wg_hbm, wu_hbm, wd_hbm, out_ref,
           wg, wu, wd, xall, meta, slot_c, wgt_c, rows, s1, r1, keep, s2, r2, hid, acc,
           rs_s, rs_r, rs_l,
           wsem, ag_s, ag_r, p_s, p_r, q_s, q_r, h_s, h_r, f_s, f_r, t_s, t_r):
    E, DP, EL, NCH, G, CAP, NB, HALF, CT = dims
    M = DP // 2
    tok, width = tok_ref.shape
    H = wg.shape[2]
    hb = H // DP
    R, T = G * CAP, G * tok
    N = EL * NCH
    ct = CT
    chunks = range(width // ct)
    n_items = N + 2 * HALF
    e = lax.axis_index("expert")
    d = lax.axis_index("dp")
    x, c = lax.div(d, 2), lax.rem(d, 2)
    mate = 2 * x + 1 - c
    has_left, has_right = e > 0, e < E - 1

    def place(s):
        return lax.rem(s + E // 4, E)

    def across(k):
        return lax.rem(x + k, M)

    def source(k):
        return lax.rem(x + M - k, M)

    def w_gu(j, slot):
        return (pltpu.make_async_copy(wg_hbm.at[j], wg.at[slot], wsem.at[0, slot]),
                pltpu.make_async_copy(wu_hbm.at[j], wu.at[slot], wsem.at[1, slot]))

    def w_d(j, slot):
        return pltpu.make_async_copy(wd_hbm.at[j], wd.at[slot], wsem.at[2, slot])

    for j in range(NB):
        for copy in w_gu(j, j):
            copy.start()
    for j in range(NB):
        w_d(j, j).start()

    barrier = pltpu.get_barrier_semaphore()

    @pl.when(has_left)
    def _():
        pl.semaphore_signal(barrier, inc=1, device_id={"expert": e - 1}, device_id_type=MESH)

    @pl.when(has_right)
    def _():
        pl.semaphore_signal(barrier, inc=1, device_id={"expert": e + 1}, device_id_type=MESH)

    pl.semaphore_signal(barrier, inc=1, device_id={"dp": mate}, device_id_type=MESH)
    for k in range(1, M):
        pl.semaphore_signal(
            barrier, inc=1, device_id={"dp": 2 * across(k) + c}, device_id_type=MESH)

    n_exp = E * EL
    affinity = 1.0 / (1.0 + jnp.exp(-sco_ref[...]))
    weights = 2.5 * affinity / jnp.sum(affinity, axis=0, keepdims=True)
    number = lax.broadcasted_iota(jnp.int32, (n_exp, tok), 0)
    routed = jnp.zeros((n_exp, tok), F32)
    weight = jnp.zeros((n_exp, tok), F32)
    for k in range(ids_ref.shape[0]):
        hit = ids_ref[k:k + 1, :] == number
        routed = routed + jnp.where(hit, 1.0, 0.0)
        weight = weight + jnp.where(hit, weights[k:k + 1, :], 0.0)
    earlier = (lax.broadcasted_iota(jnp.int32, (tok, tok), 0)
               < lax.broadcasted_iota(jnp.int32, (tok, tok), 1))
    rank = dot(routed.astype(BF16), jnp.where(earlier, 1.0, 0.0).astype(BF16))
    base = (place(e) * CAP).astype(F32)
    meta[e, :, :tok] = jnp.where(routed > 0.5, rank + base, -1.0)
    meta[e, :, tok:] = weight
    xall[place(e)] = tok_ref[...]

    pl.semaphore_wait(barrier, M + has_left.astype(jnp.int32) + has_right.astype(jnp.int32))

    def gather_to(s, side, target):
        return (remote(meta.at[s], meta.at[s], ag_s.at[side, 0, s], ag_r.at[0, s], expert=target),
                remote(xall.at[place(s)], xall.at[place(s)], ag_s.at[side, 1, s], ag_r.at[1, s], expert=target))

    def start_right(s):
        @pl.when(has_right)
        def _():
            for copy in gather_to(s, 0, e + 1):
                copy.start()

    def start_left(s):
        @pl.when(has_left)
        def _():
            for copy in gather_to(s, 1, e - 1):
                copy.start()

    start_right(e)
    start_left(e)

    def gather_step(k, carry):
        @pl.when(e - k >= 0)
        def _():
            for copy in gather_to(e - k, 0, e):
                copy.wait_recv()
            start_right(e - k)

        @pl.when(e + k <= E - 1)
        def _():
            for copy in gather_to(e + k, 1, e):
                copy.wait_recv()
            start_left(e + k)

        return carry

    def list_slots(places):
        for p in places:
            own = meta[(p + E - E // 4) % E, pl.ds(e * EL, EL), :]
            lanes = slice(p % 2 * tok, (p % 2 + 1) * tok)
            slot_c[p // 2, :, lanes] = own[:, :tok]
            wgt_c[p // 2, :, lanes] = own[:, tok:]

    if HALF:
        lax.fori_loop(1, 3 * E // 4, gather_step, 0)
        list_slots(range(E // 2, E))
    else:
        lax.fori_loop(1, E, gather_step, 0)
        list_slots(range(E))
    acc[...] = jnp.zeros_like(acc)

    class Item:
        def __init__(self, j, q, parts, first, last):
            self.j, self.q, self.first, self.last = j, q, first, last
            self.group = G // parts
            self.rows, self.toks = R // parts, T // parts
            self.start = q * self.group
            if parts == 1:
                self.buf = j if NCH == 1 else j * NCH + q
                self.sem = 2 * self.buf
                self.span = pl.ds(0, R)
            else:
                self.buf, self.sem = j, 2 * j + q
                self.span = pl.ds(pl.multiple_of(q * self.rows, self.rows), self.rows)
            self.places = pl.ds(self.start, self.group)

        def row(self, table):
            pairs = self.group // 2
            return jnp.concatenate(
                [table[self.q * pairs + p, pl.ds(self.j, 1), :] for p in range(pairs)], axis=1)

    def taken(it):
        row = it.row(slot_c)
        first = it.start * CAP
        return (row.astype(jnp.int32) - first
                == lax.broadcasted_iota(jnp.int32, (it.rows, it.toks), 0))

    def pair_copy(it):
        return remote(s1.at[it.buf, :, it.span], r1.at[it.buf, :, it.span],
                      p_s.at[it.sem], p_r.at[it.sem], dp=mate)

    def sum_copy(it, k):
        return remote(s2.at[it.buf, across(k), it.span], r2.at[it.buf, x, it.span],
                      q_s.at[it.sem, k], q_r.at[it.sem, k], dp=2 * across(k) + c)

    def share_copy(it, k):
        return remote(hid.at[it.buf, d, it.span], hid.at[it.buf, d, it.span],
                      h_s.at[it.sem, k], h_r.at[it.sem, k], dp=2 * across(k) + c)

    def mate_copy(it, k):
        block = 2 * source(k) + c
        return remote(hid.at[it.buf, block, it.span], hid.at[it.buf, block, it.span],
                      f_s.at[it.sem, k], f_r.at[it.sem, k], dp=mate)

    def stage_a(it):
        j, span = it.j, it.span
        slot = lax.rem(j, NB)

        @pl.when(it.first)
        def _():
            for copy in w_gu(j, slot):
                copy.wait()

        pick = jnp.where(taken(it), 1.0, 0.0).astype(BF16)
        for at in range(0, width, ct):
            xq = xall[it.places, :, at:at + ct].reshape(it.toks, ct)
            rows[:it.rows, at:at + ct] = dot(pick, xq).astype(BF16)

        def block(m, core):
            cols = pl.ds(pl.multiple_of((2 * m + core) * hb, hb), hb)
            xr = rows[:it.rows, :]
            return dot(xr, wg[slot, :, cols]), dot(xr, wu[slot, :, cols])

        for m in range(M):
            g, u = block(m, 1 - c)
            s1[it.buf, m, span, :hb] = g.astype(BF16)
            s1[it.buf, m, span, hb:] = u.astype(BF16)
        pair_copy(it).start()
        for m in range(M):
            g, u = block(m, c)
            keep[it.buf, m, span, :hb] = g
            keep[it.buf, m, span, hb:] = u

        @pl.when(it.last & (j + NB < EL))
        def _():
            for copy in w_gu(j + NB, slot):
                copy.start()

    def stage_b(it):
        i, span = it.buf, it.span
        pair_copy(it).wait_recv()
        for k in range(1, M):
            to = across(k)
            s2[i, to, span] = (keep[i, to, span] + r1[i, to, span].astype(F32)).astype(BF16)
            sum_copy(it, k).start()
        keep[i, x, span] = keep[i, x, span] + r1[i, x, span].astype(F32)

    def stage_c(it):
        i, span = it.buf, it.span
        total = keep[i, x, span]
        for k in range(1, M):
            sum_copy(it, k).wait_recv()
            total = total + r2[i, source(k), span].astype(F32)
        g, u = total[:, :hb], total[:, hb:]
        hid[i, d, span] = (g / (1.0 + jnp.exp(-g)) * u).astype(BF16)
        for k in range(1, M):
            share_copy(it, k).start()
        mate_copy(it, 0).start()

    def stage_d(it):
        for k in range(1, M):
            share_copy(it, k).wait_recv()
            mate_copy(it, k).start()

    def stage_e(it):
        j, span = it.j, it.span
        slot = lax.rem(j, NB)

        @pl.when(it.first)
        def _():
            w_d(j, slot).wait()

        for k in range(M):
            mate_copy(it, k).wait_recv()
        hit = taken(it)
        scale = jnp.sum(jnp.where(hit, it.row(wgt_c), 0.0),
                        axis=1, keepdims=True)
        pick = jnp.where(hit, 1.0, 0.0).astype(BF16)
        hidden = jnp.concatenate([hid[it.buf, b, span] for b in range(DP)], axis=1)
        for at in range(0, width, ct):
            out = (dot(hidden, wd[slot, :, at:at + ct]) * scale).astype(BF16)
            add = dot(pick, out, ((0,), (0,))).reshape(it.group, tok, ct)
            acc[it.places, :, at:at + ct] += add

        @pl.when(it.last & (j + NB < EL))
        def _():
            w_d(j + NB, slot).start()

    def tail_right(s, n, target):
        return remote(rs_s.at[s, n], rs_r.at[s, n], t_s.at[s, n], t_r.at[0, s, n], expert=target)

    def tail_left(s, n, target):
        return remote(rs_s.at[s, n], rs_l.at[s, n], t_s.at[s, n], t_r.at[1, s, n], expert=target)

    def first_sums(s, copy_to, target):
        for n in chunks:
            rs_s[s, n] = acc[place(s), :, n * ct:(n + 1) * ct].astype(BF16)
            copy_to(s, n, target).start()

    def outer_sums():
        @pl.when(jnp.logical_not(has_left))
        def _():
            first_sums(E - 1, tail_right, e + 1)

        @pl.when(jnp.logical_not(has_right))
        def _():
            first_sums(0, tail_left, e - 1)

    stages = (stage_a, stage_b, stage_c, stage_d, stage_e)

    n_ends = n_items - 2 * HALF

    def on_item(t, stage):
        if HALF == 0:
            if NCH == 1:
                stage(Item(t, 0, 1, t >= 0, t >= 0))
            else:
                q = lax.rem(t, NCH)
                stage(Item(lax.div(t, NCH), q, 1, q == 0, q == NCH - 1))
            return
        in_full = (t >= 2 * HALF) & (t < n_ends)

        @pl.when(in_full)
        def _():
            stage(Item(t - HALF, 0, 1, t >= 0, t >= 0))

        @pl.when(jnp.logical_not(in_full))
        def _():
            end = lax.div(t, n_ends)
            u = t - end * n_ends
            turn = lax.div(u, HALF)
            j = lax.rem(u, HALF) + end * (EL - HALF)
            q = end * turn + (1 - end) * (1 - turn)
            stage(Item(j, q, 2, turn == 0, turn == 1))

    def step(i, carry):
        if HALF:
            @pl.when(i == HALF)
            def _():
                lax.fori_loop(3 * E // 4, E, gather_step, 0)
                list_slots(range(E // 2))

        for stage, lag in zip(stages, LAGS):
            @pl.when((i >= lag) & (i < n_items + lag))
            def _(stage=stage, lag=lag):
                on_item(i - lag, stage)
        if HALF:
            @pl.when(i == n_items - HALF - 1 + LAGS[-1])
            def _():
                outer_sums()
        return carry

    lax.fori_loop(0, n_items + LAGS[-1], step, 0)

    if not HALF:
        outer_sums()

    def tail_step(t, carry):
        far, near = E - 1 - t, t
        for n in chunks:
            cols = slice(n * ct, (n + 1) * ct)

            @pl.when((far > e) & has_left)
            def _():
                tail_right(far, n, e).wait_recv()
                rs_s[far, n] = (acc[place(far), :, cols] + rs_r[far, n].astype(F32)).astype(BF16)
                tail_right(far, n, e + 1).start()

            @pl.when((far > e) & jnp.logical_not(has_left) & (t > 0))
            def _():
                rs_s[far, n] = acc[place(far), :, cols].astype(BF16)
                tail_right(far, n, e + 1).start()

            @pl.when((near < e) & has_right)
            def _():
                tail_left(near, n, e).wait_recv()
                rs_s[near, n] = (acc[place(near), :, cols]
                                 + rs_l[near, n].astype(F32)).astype(BF16)
                tail_left(near, n, e - 1).start()

            @pl.when((near < e) & jnp.logical_not(has_right) & (t > 0))
            def _():
                rs_s[near, n] = acc[place(near), :, cols].astype(BF16)
                tail_left(near, n, e - 1).start()

        return carry

    lax.fori_loop(0, E - 1, tail_step, 0)

    for n in chunks:
        cols = slice(n * ct, (n + 1) * ct)

        @pl.when(has_left)
        def _():
            tail_right(e, n, e).wait_recv()
            acc[place(e), :, cols] = acc[place(e), :, cols] + rs_r[e, n].astype(F32)

        @pl.when(has_right)
        def _():
            tail_left(e, n, e).wait_recv()
            acc[place(e), :, cols] = acc[place(e), :, cols] + rs_l[e, n].astype(F32)

        out_ref[:, cols] = acc[place(e), :, cols].astype(BF16)

    def drain_line(s, carry):
        @pl.when((s <= e) & has_right)
        def _():
            for copy in gather_to(s, 0, e):
                copy.wait_send()

        @pl.when((s >= e) & has_left)
        def _():
            for copy in gather_to(s, 1, e):
                copy.wait_send()

        @pl.when(s != e)
        def _():
            for n in chunks:
                tail_right(s, n, e).wait_send()

        return carry

    lax.fori_loop(0, E, drain_line, 0)

    def drain(it):
        pair_copy(it).wait_send()
        mate_copy(it, 0).wait_send()
        for k in range(1, M):
            sum_copy(it, k).wait_send()
            share_copy(it, k).wait_send()
            mate_copy(it, k).wait_send()

    def drain_item(t, carry):
        on_item(t, drain)
        return carry

    lax.fori_loop(0, n_items, drain_item, 0)


def on_device(tokens, expert_ids, scores, w_gate, w_up, w_down):
    E, DP = lax.axis_size("expert"), lax.axis_size("dp")
    tok, width = tokens.shape
    top = expert_ids.shape[1]
    EL, _, H = w_gate.shape
    n_exp = E * EL
    CAP = 2 * tok * top // n_exp
    G = min(E, 4)
    NCH = E // G
    NB = min(3, EL)
    HALF = 2 if NCH == 1 and G == 4 and EL > 4 else 0
    ct = tile_of(width)
    tail = (E, width // ct, tok, ct)
    M, hb, R, N = DP // 2, H // DP, G * CAP, EL * NCH
    vmem, dma = pltpu.VMEM, pltpu.SemaphoreType.DMA
    scratch = [
        vmem((NB, width, H), BF16), vmem((NB, width, H), BF16), vmem((NB, H, width), BF16),
        vmem((E, tok, width), BF16), vmem((E, n_exp, 2 * tok), F32),
        vmem((E // 2, EL, 2 * tok), F32), vmem((E // 2, EL, 2 * tok), F32),
        vmem((R, width), BF16),
        vmem((N, M, R, 2 * hb), BF16), vmem((N, M, R, 2 * hb), BF16),
        vmem((N, M, R, 2 * hb), F32),
        vmem((N, M, R, 2 * hb), BF16), vmem((N, M, R, 2 * hb), BF16),
        vmem((N, DP, R, hb), BF16),
        vmem((E, tok, width), F32),
        vmem(tail, BF16), vmem(tail, BF16), vmem(tail, BF16),
        dma((3, NB)), dma((2, 2, E)), dma((2, E)),
        dma((2 * N,)), dma((2 * N,)), dma((2 * N, M)), dma((2 * N, M)), dma((2 * N, M)),
        dma((2 * N, M)), dma((2 * N, M)), dma((2 * N, M)),
        dma((E, width // ct)), dma((2, E, width // ct)),
    ]
    whole = pl.BlockSpec(memory_space=pltpu.VMEM)
    hbm = pl.BlockSpec(memory_space=pl.ANY)
    return pl.pallas_call(
        functools.partial(kernel, (E, DP, EL, NCH, G, CAP, NB, HALF, ct)),
        out_shape=jax.ShapeDtypeStruct((tok, width), BF16),
        in_specs=[whole] * 3 + [hbm] * 3,
        out_specs=whole,
        scratch_shapes=scratch,
        compiler_params=pltpu.CompilerParams(
            collective_id=0, has_side_effects=True, vmem_limit_bytes=60 * 2**20),
        name="routed_experts",
    )(tokens, expert_ids.T, scores.T, w_gate, w_up, w_down)


def solution(mesh):
    in_specs = (
        P(("groups", "expert"), "dp"),
        P(("groups", "expert"), None),
        P(("groups", "expert"), None),
        P("expert", "dp", None),
        P("expert", "dp", None),
        P("expert", None, "dp"),
    )
    out_specs = P(("groups", "expert"), "dp")
    return jax.shard_map(
        on_device, mesh=mesh, in_specs=in_specs, out_specs=out_specs, check_vma=False
    )
```

time: 91.8 us -> 97.6 us (1.063)
  Pallas kernels: 90 us -> 95.8 us
    pallas_call x1, Pallas kernels: 90 us -> 95.8 us  [on_device(): pl.pallas_call(functools.partial(kernel, (E, DP, EL, NCH, G, CAP, NB, HAL...]
where the time goes in v2:
time: 97.6 us; the launch traced here: 97.5 us
  Pallas kernels  95.8 us (98%)
  local copies, waits for them, and re-layouts  1.62 us (2%)
    pallas_call x1, Pallas kernels, on_device(): pl.pallas_call(functools.partial(kernel, (E, DP, EL, NCH, G, CAP, NB, HAL...  95.8 us

profile of v2, /device:TPU:0, one launch (start us, length us, event | category | flops | bytes accessed | tf_op | source)
XLA Modules:
  0.0 97.5 jit_solution(9238427651312609351)
XLA Ops:
  0.0 95.8 %routed_experts.1 = bf16[64,1536]{1,0:T(8,128)(2,1)} custom-call(bf16[64,1536]{1,0:T(8,128)(2,1)} %tok_ref.1, s32[8,64]{1,0:T(8,128)} %bitcast.2, f32[8,64]{1,0:T(8,128)} %bitcast.3, bf16[8,1536,1024]{2,1,0:T(8,128)(2,1)} %wg_hbm.1, bf16[8,1536,1024]{2,1,0:T(8,128)(2,1)} %wu_hbm.1, bf16[8,1024,1536]{2,1,0:T(8,128)(2,1)} %wd_hbm.1), custom_call_target="tpu_custom_call" | custom-call | tf_op jit(solution)/shard_map/routed_experts/pallas_call | solution.py:470
  95.8 1.6 %copy.8 = bf16[64,1536]{1,0:T(8,128)(2,1)} copy(bf16[64,1536]{1,0:T(8,128)(2,1)} %routed_experts.1) | data formatting | bytes 393216

commit v3 on v2

--- a/solution.py
+++ b/solution.py
@@ -9,7 +9,7 @@
 
 MESH = pl.DeviceIdType.MESH
 F32, BF16 = jnp.float32, jnp.bfloat16
-LAGS = (0, 1, 2, 3, 4)
+LAGS = (0, 1, 3, 5, 7)
 
 
 def dot(a, b, dims=((1,), (0,))):
@@ -34,7 +34,7 @@
            wg, wu, wd, xall, meta, slot_c, wgt_c, rows, s1, r1, keep, s2, r2, hid, acc,
            rs_s, rs_r, rs_l,
            wsem, ag_s, ag_r, p_s, p_r, q_s, q_r, h_s, h_r, f_s, f_r, t_s, t_r):
-    E, DP, EL, NCH, G, CAP, NB, HALF, CT = dims
+    E, DP, EL, NCH, G, CAP, NB, HALF, CT, tw = dims
     M = DP // 2
     tok, width = tok_ref.shape
     H = wg.shape[2]
@@ -42,7 +42,7 @@
     R, T = G * CAP, G * tok
     N = EL * NCH
     ct = CT
-    chunks = range(width // ct)
+    chunks = range(width // tw)
     n_items = N + 2 * HALF
     e = lax.axis_index("expert")
     d = lax.axis_index("dp")
@@ -291,7 +291,7 @@
 
     def first_sums(s, copy_to, target):
         for n in chunks:
-            rs_s[s, n] = acc[place(s), :, n * ct:(n + 1) * ct].astype(BF16)
+            rs_s[s, n] = acc[place(s), :, n * tw:(n + 1) * tw].astype(BF16)
             copy_to(s, n, target).start()
 
     def outer_sums():
@@ -355,7 +355,7 @@
     def tail_step(t, carry):
         far, near = E - 1 - t, t
         for n in chunks:
-            cols = slice(n * ct, (n + 1) * ct)
+            cols = slice(n * tw, (n + 1) * tw)
 
             @pl.when((far > e) & has_left)
             def _():
@@ -385,7 +385,7 @@
     lax.fori_loop(0, E - 1, tail_step, 0)
 
     for n in chunks:
-        cols = slice(n * ct, (n + 1) * ct)
+        cols = slice(n * tw, (n + 1) * tw)
 
         @pl.when(has_left)
         def _():
@@ -446,7 +446,8 @@
     NB = min(3, EL)
     HALF = 2 if NCH == 1 and G == 4 and EL > 4 else 0
     ct = tile_of(width)
-    tail = (E, width // ct, tok, ct)
+    tw = width
+    tail = (E, width // tw, tok, tw)
     M, hb, R, N = DP // 2, H // DP, G * CAP, EL * NCH
     vmem, dma = pltpu.VMEM, pltpu.SemaphoreType.DMA
     scratch = [
@@ -463,12 +464,12 @@
         dma((3, NB)), dma((2, 2, E)), dma((2, E)),
         dma((2 * N,)), dma((2 * N,)), dma((2 * N, M)), dma((2 * N, M)), dma((2 * N, M)),
         dma((2 * N, M)), dma((2 * N, M)), dma((2 * N, M)),
-        dma((E, width // ct)), dma((2, E, width // ct)),
+        dma((E, width // tw)), dma((2, E, width // tw)),
     ]
     whole = pl.BlockSpec(memory_space=pltpu.VMEM)
     hbm = pl.BlockSpec(memory_space=pl.ANY)
     return pl.pallas_call(
-        functools.partial(kernel, (E, DP, EL, NCH, G, CAP, NB, HALF, ct)),
+        functools.partial(kernel, (E, DP, EL, NCH, G, CAP, NB, HALF, ct, tw)),
         out_shape=jax.ShapeDtypeStruct((tok, width), BF16),
         in_specs=[whole] * 3 + [hbm] * 3,
         out_specs=whole,

time: 97.6 us -> 87.1 us (0.89)
  Pallas kernels: 95.8 us -> 85.3 us
    pallas_call x1, Pallas kernels: 95.8 us -> 85.3 us  [on_device(): pl.pallas_call(functools.partial(kernel, (E, DP, EL, NCH, G, CAP, NB, HAL...]
where the time goes in v3:
time: 87.1 us; the launch traced here: 86.9 us
  Pallas kernels  85.3 us (98%)
  local copies, waits for them, and re-layouts  1.62 us (2%)
    pallas_call x1, Pallas kernels, on_device(): pl.pallas_call(functools.partial(kernel, (E, DP, EL, NCH, G, CAP, NB, HAL...  85.3 us

profile of v3, /device:TPU:0, one launch (start us, length us, event | category | flops | bytes accessed | tf_op | source)
XLA Modules:
  0.0 86.9 jit_solution(13508919637118717366)
XLA Ops:
  0.0 85.3 %routed_experts.1 = bf16[64,1536]{1,0:T(8,128)(2,1)} custom-call(bf16[64,1536]{1,0:T(8,128)(2,1)} %tok_ref.1, s32[8,64]{1,0:T(8,128)} %bitcast.2, f32[8,64]{1,0:T(8,128)} %bitcast.3, bf16[8,1536,1024]{2,1,0:T(8,128)(2,1)} %wg_hbm.1, bf16[8,1536,1024]{2,1,0:T(8,128)(2,1)} %wu_hbm.1, bf16[8,1024,1536]{2,1,0:T(8,128)(2,1)} %wd_hbm.1), custom_call_target="tpu_custom_call" | custom-call | tf_op jit(solution)/shard_map/routed_experts/pallas_call | solution.py:471
  85.3 1.6 %copy.8 = bf16[64,1536]{1,0:T(8,128)(2,1)} copy(bf16[64,1536]{1,0:T(8,128)(2,1)} %routed_experts.1) | data formatting | bytes 393216
